TPU v7x, 256 devices: a whole 4x4x8 slice. The times are simulated.
256 devices in a mesh: section: 16 (over z_lo, x), ctx: 16 (over z_hi, y, core).
Axes of the slice: x: 4, y: 4, z: 8 (z_hi: 2, z_lo: 4; z = z_hi * 4 + z_lo), core: 2. Of those that a mesh axis runs over, the one named last changes fastest.
Arguments:
- queries: bfloat16 [16, 4096, 16, 128], P('section', 'ctx'), may hold values from -12 to 12
- keys: bfloat16 [16, 4096, 128], P('section', 'ctx'), may hold values from -6 to 6
- values: bfloat16 [16, 4096, 128], P('section', 'ctx'), may hold values from -6 to 6
- outputs: bfloat16 [16, 4096, 16, 128], P('section', 'ctx'), may hold values from -6 to 6, as said below
- grad_held: bfloat16 [16, 4096, 16, 128], P('section', 'ctx'), may hold values from -24 to 24
- lse: float32 [16, 16, 4096], P('section', None, 'ctx'), as said below
- span_start: int32 [32], replicated, may hold values from 0 to 3968, as said below
Outputs:
- query_grad: bfloat16 [16, 4096, 16, 128], P('section', 'ctx')
- key_grad: bfloat16 [16, 4096, 128], P('section', 'ctx')
- value_grad: bfloat16 [16, 4096, 128], P('section', 'ctx')
Inputs may be any that keep to these rules, and one draw needn't show every extreme that they name: `span_start`: each multiple of 128 below 4096 appears once. Entries 2 k and 2 k + 1 are the spans held by index k of ctx; they add up to 3968, the smaller first. lse[s, h, i] is the log of the sum of exp(scores[s, h, i, j]) over the j with positions[j] <= positions[i]. outputs[s, i, h] is the sum over j of probs[s, h, i, j] values[s, j], rounded once.
All inputs are finite; a program needn't handle non-finite values.
Results may differ from a plain program's by a relative error of at most 0.014.
Values may be sent and summed in bfloat16 or wider, within the bound.
A program may use at most 64 MiB of HBM per device.

v0:
```python
import jax
import jax.numpy as jnp
from jax import lax
from jax.sharding import PartitionSpec as P


def from_behind(shard, axis, by):
    length = lax.axis_size(axis)
    return lax.ppermute(shard, axis, [(i, (i + by) % length) for i in range(length)])


def tile_grads(
    query_rows, grad_rows, lse_rows, delta_rows, query_pos, key_rows, value_rows, key_pos
):
    score_scale = query_rows.shape[-1] ** (-0.5)
    scores = (
        jnp.einsum("rhd,cd->hrc", query_rows, key_rows, preferred_element_type=jnp.float32)
        * score_scale
    )
    allowed = key_pos[None, :] <= query_pos[:, None]
    probs = jnp.where(allowed[None], jnp.exp(scores - lse_rows[:, :, None]), 0.0)
    probs_low = probs.astype(jnp.bfloat16)
    grad_probs = jnp.einsum(
        "rhd,cd->hrc", grad_rows, value_rows, preferred_element_type=jnp.float32
    )
    grad_scores = (probs * (grad_probs - delta_rows[:, :, None])).astype(jnp.bfloat16)
    query_grad = (
        jnp.einsum("hrc,cd->rhd", grad_scores, key_rows, preferred_element_type=jnp.float32)
        * score_scale
    )
    key_grad = (
        jnp.einsum("hrc,rhd->cd", grad_scores, query_rows, preferred_element_type=jnp.float32)
        * score_scale
    )
    value_grad = jnp.einsum("hrc,rhd->cd", probs_low, grad_rows, preferred_element_type=jnp.float32)
    return (query_grad, key_grad, value_grad)


def full_tile(operands):
    return tile_grads(
        operands[0],
        operands[1],
        operands[2],
        operands[3],
        operands[4],
        operands[5],
        operands[6],
        operands[7],
    )


def empty_grads(operands):
    query_rows = operands[0]
    key_rows = operands[5]
    return (
        jnp.zeros(query_rows.shape, jnp.float32),
        jnp.zeros(key_rows.shape, jnp.float32),
        jnp.zeros(key_rows.shape, jnp.float32),
    )


def sweep_keys(query_side, key_rows, value_rows):
    queries, grad_out, lse_rows, delta_rows, query_pos, own_starts, span_start = query_side
    row_count = queries.shape[0]
    span_rows = row_count // 2
    head_size = key_rows.shape[1]
    block_count = key_rows.shape[0] // row_count
    offsets = jnp.arange(span_rows, dtype=jnp.int32)
    query_init = jnp.zeros(queries.shape, jnp.float32)
    keys_init = jnp.zeros((key_rows.shape[0], 2 * head_size), jnp.float32)

    def sweep_turn(block_index, totals):
        query_total, key_total = totals
        key_block = lax.dynamic_slice_in_dim(key_rows, block_index * row_count, row_count, 0)
        value_block = lax.dynamic_slice_in_dim(value_rows, block_index * row_count, row_count, 0)
        block_starts = lax.dynamic_slice_in_dim(
            span_start, block_index * row_count // span_rows, 2, 0
        )
        query_parts = []
        key_parts = [
            jnp.zeros((span_rows, head_size), jnp.float32),
            jnp.zeros((span_rows, head_size), jnp.float32),
        ]
        value_parts = [
            jnp.zeros((span_rows, head_size), jnp.float32),
            jnp.zeros((span_rows, head_size), jnp.float32),
        ]
        for query_half in range(2):
            row_low = query_half * span_rows
            row_high = row_low + span_rows
            query_sum = jnp.zeros((span_rows,) + queries.shape[1:], jnp.float32)
            for key_half in range(2):
                key_low = key_half * span_rows
                key_high = key_low + span_rows
                operands = (
                    queries[row_low:row_high],
                    grad_out[row_low:row_high],
                    lse_rows[:, row_low:row_high],
                    delta_rows[:, row_low:row_high],
                    query_pos[row_low:row_high],
                    key_block[key_low:key_high],
                    value_block[key_low:key_high],
                    block_starts[key_half] + offsets,
                )
                tile_out = lax.cond(
                    block_starts[key_half] <= own_starts[query_half],
                    full_tile,
                    empty_grads,
                    operands,
                )
                query_sum = query_sum + tile_out[0]
                key_parts[key_half] = key_parts[key_half] + tile_out[1]
                value_parts[key_half] = value_parts[key_half] + tile_out[2]
            query_parts.append(query_sum)
        query_grad = jnp.concatenate(query_parts, axis=0)
        key_grad = jnp.concatenate(key_parts, axis=0)
        value_grad = jnp.concatenate(value_parts, axis=0)
        query_total = query_total + query_grad
        key_total = lax.dynamic_update_slice_in_dim(
            key_total, jnp.concatenate([key_grad, value_grad], axis=1), block_index * row_count, 0
        )
        return (query_total, key_total)

    return lax.fori_loop(0, block_count, sweep_turn, (query_init, keys_init))


def body(queries, keys, values, outputs, grad_held, lse, span_start):
    grad_next = from_behind(grad_held, "section", -1)
    query_block = queries[0]
    key_block = keys[0]
    value_block = values[0]
    row_count = query_block.shape[0]
    span_rows = row_count // 2
    head_size = key_block.shape[1]
    context = lax.axis_index("ctx")
    own_starts = lax.dynamic_slice_in_dim(span_start, 2 * context, 2, 0)
    offsets = jnp.arange(span_rows, dtype=jnp.int32)
    query_pos = (own_starts[:, None] + offsets[None, :]).reshape(row_count)
    grad_out = grad_next[0]
    delta_rows = jnp.sum(grad_out.astype(jnp.float32) * outputs[0].astype(jnp.float32), axis=-1).T
    query_side = (query_block, grad_out, lse[0], delta_rows, query_pos, own_starts, span_start)
    query_add, key_value_part = sweep_keys(
        query_side,
        lax.all_gather(key_block, "ctx", axis=0, tiled=True),
        lax.all_gather(value_block, "ctx", axis=0, tiled=True),
    )
    key_value_full = key_value_part
    query_total, key_value_full = (query_add, key_value_full)
    summed = lax.psum_scatter(
        key_value_full.astype(jnp.bfloat16), "ctx", scatter_dimension=0, tiled=True
    ).astype(jnp.float32)
    query_out = query_total.astype(jnp.bfloat16)[None]
    key_out = summed[:, :head_size].astype(jnp.bfloat16)[None]
    value_out = summed[:, head_size:].astype(jnp.bfloat16)[None]
    return (query_out, key_out, value_out)


def solution(mesh):
    placed = (
        P("section", "ctx", None, None),
        P("section", "ctx", None),
        P("section", "ctx", None),
        P("section", "ctx", None, None),
        P("section", "ctx", None, None),
        P("section", None, "ctx"),
        P(),
    )
    return jax.shard_map(
        body,
        mesh=mesh,
        in_specs=placed,
        out_specs=(
            P("section", "ctx", None, None),
            P("section", "ctx", None),
            P("section", "ctx", None),
        ),
        check_vma=False,
    )
```

profile of v0, /device:TPU:2, one launch (start us, length us, event | category | flops | bytes accessed | tf_op | source)
XLA Modules:
  0.0 635.1 jit_solution(2357705479401431310)
XLA Ops:
  8.7 2.6 copy.15
  17.2 19.2 %collective-permute-done = bf16[1,256,16,128]{3,1,2,0:T(8,128)(2,1)S(1)} collective-permute-done((bf16[1,256,16,128]{3,1,2,0:T(8,128)(2,1)}, bf16[1,256,16,128]{3,1,2,0:T(8,128)(2,1)S(1)}, u32[]{:S(2)}, u32[]{:S(2)}) %collective-permute-start) | collective-permute-done | bytes 1048608 | tf_op jit(solution)/shard_map/ppermute | solution.py:9
  37.1 44.0 %all-gather.5.cloned.1.call-done = bf16[1,4096,128]{2,1,0:T(8,128)(2,1)} async-done(((bf16[1,256,128]{2,1,0:T(8,128)(2,1)}), bf16[1,4096,128]{2,1,0:T(8,128)(2,1)}) %all-gather.5.cloned.1.call-update) | async-done | bytes 1048592 | tf_op jit(solution)/shard_map/all_gather | solution.py:144
  81.1 53.9 %all-gather.7.cloned.1.call-done = bf16[1,4096,128]{2,1,0:T(8,128)(2,1)} async-done(((bf16[1,256,128]{2,1,0:T(8,128)(2,1)}), bf16[1,4096,128]{2,1,0:T(8,128)(2,1)}) %all-gather.7.cloned.1.call-update) | async-done | bytes 1048592 | tf_op jit(solution)/shard_map/all_gather | solution.py:145
  136.5 407.7 %while.19 = (s32[]{:T(128)}, f32[256,16,128]{2,0,1:T(8,128)}, bf16[4096,256]{1,0:T(8,128)(2,1)}, s32[32]{0:T(128)}, s32[2]{0:T(128)}, /*index=5*/bf16[4096,128]{...) while((s32[]{:T(128)}, f32[256,16,128]{2,0,1:T(8,128)}, ...), condition=%wide.region_10.11_spmd.clone.clone, body=%wide.region_1.10_spmd.clone.clone.sunk | while | flops 1353384192 | bytes 84388064 | solution.py:124
  154.0 2.4 conditional.16
  181.9 2.4 conditional.17
  204.9 2.4 conditional.16
  207.3 2.4 conditional.17
  232.7 2.4 conditional.17
  255.7 2.4 conditional.16
  258.2 2.4 conditional.17
  283.6 2.4 conditional.17
  306.6 2.4 conditional.16
  334.4 2.4 conditional.17
  357.5 2.4 conditional.16
  385.3 2.4 conditional.17
  408.3 2.4 conditional.16
  435.3 2.4 conditional.16
  460.9 2.4 conditional.17
  486.4 2.4 conditional.17
  509.4 2.4 conditional.16
  537.2 2.4 conditional.17
  548.0 79.1 %reduce-scatter.2.cloned.1.call-done = bf16[256,256]{1,0:T(8,128)(2,1)} async-done(((bf16[4096,256]{1,0:T(8,128)(2,1)}), bf16[256,256]{1,0:T(8,128)(2,1)}) %reduce-scatter.2.cloned.1.call-update) | async-done | bytes 131088 | tf_op jit(solution)/shard_map/reduce_scatter | solution.py:149
  (936 shorter events, 369.9 us)
Async XLA Ops:
  7.2 73.9 %all-gather.5.cloned.1.call-start = ((), (), s32[]{:S(2)}) async-start(), calls=%async_computation.2 | async-start | bytes 1114112 | tf_op jit(solution)/shard_map/all_gather | solution.py:144
  7.9 127.1 %all-gather.7.cloned.1.call-start = ((), (), s32[]{:S(2)}) async-start(), calls=%async_computation.3 | async-start | bytes 1114112 | tf_op jit(solution)/shard_map/all_gather | solution.py:145
  8.7 27.7 %copy-start.9 = (bf16[1,256,16,128]{3,2,1,0:T(8,128)(2,1)S(1)}, bf16[1,256,16,128]{3,2,1,0:T(8,128)(2,1)}, u32[]{:S(2)}) copy-start(bf16[1,256,16,128]{3,2,1,0:T(8,128)(2,1)} %param.20) | copy-start | bytes 3145732
  8.7 618.4 %reduce-scatter.2.cloned.1.call-start = ((), (), s32[]{:S(2)}) async-start(), calls=%async_computation.1 | async-start | bytes 2228224 | tf_op jit(solution)/shard_map/reduce_scatter | solution.py:149
  11.3 25.1 %collective-permute-start = (bf16[1,256,16,128]{3,1,2,0:T(8,128)(2,1)}, bf16[1,256,16,128]{3,1,2,0:T(8,128)(2,1)S(1)}, u32[]{:S(2)}, u32[]{:S(2)}) collective-permute-start(bf16[1,256,16,128]{3,1,2,0:T(8,128)(2,1)} %copy.15), channel_id=1, source_target_pairs={{0,240},{16,0},{32,16},{48,32},{64,48},{80,64},{96,80},{112,96},{1... | collective-permute-start | bytes 3145736 | tf_op jit(solution)/shard_map/ppermute | solution.py:9
  17.2 119.3 %copy-start.12 = (f32[1,16,256]{2,1,0:T(8,128)S(1)}, f32[1,16,256]{2,1,0:T(8,128)}, u32[]{:S(2)}) copy-start(f32[1,16,256]{2,1,0:T(8,128)} %param.22) | copy-start | bytes 49156
  163.4 13.3 %copy-start.5 = (bf16[256,16,128]{2,0,1:T(8,128)(2,1)}, bf16[256,16,128]{2,0,1:T(8,128)(2,1)S(1)}, u32[]{:S(2)}) copy-start(bf16[256,16,128]{2,0,1:T(8,128)(2,1)S(1)} %get-tuple-element.783) | copy-start | bytes 3145732 | tf_op jit(solution)/shard_map/while
  163.4 13.3 %copy-start.10 = (f32[16,256]{1,0:T(8,128)}, f32[16,256]{1,0:T(8,128)S(1)}, u32[]{:S(2)}) copy-start(f32[16,256]{1,0:T(8,128)S(1)} %get-tuple-element.784) | copy-start | bytes 49156 | tf_op jit(solution)/shard_map/while
  188.8 13.3 %copy-start.5 = (bf16[256,16,128]{2,0,1:T(8,128)(2,1)}, bf16[256,16,128]{2,0,1:T(8,128)(2,1)S(1)}, u32[]{:S(2)}) copy-start(bf16[256,16,128]{2,0,1:T(8,128)(2,1)S(1)} %get-tuple-element.783) | copy-start | bytes 3145732 | tf_op jit(solution)/shard_map/while
  188.8 13.3 %copy-start.10 = (f32[16,256]{1,0:T(8,128)}, f32[16,256]{1,0:T(8,128)S(1)}, u32[]{:S(2)}) copy-start(f32[16,256]{1,0:T(8,128)S(1)} %get-tuple-element.784) | copy-start | bytes 49156 | tf_op jit(solution)/shard_map/while
  214.2 13.3 %copy-start.5 = (bf16[256,16,128]{2,0,1:T(8,128)(2,1)}, bf16[256,16,128]{2,0,1:T(8,128)(2,1)S(1)}, u32[]{:S(2)}) copy-start(bf16[256,16,128]{2,0,1:T(8,128)(2,1)S(1)} %get-tuple-element.783) | copy-start | bytes 3145732 | tf_op jit(solution)/shard_map/while
  214.2 13.3 %copy-start.10 = (f32[16,256]{1,0:T(8,128)}, f32[16,256]{1,0:T(8,128)S(1)}, u32[]{:S(2)}) copy-start(f32[16,256]{1,0:T(8,128)S(1)} %get-tuple-element.784) | copy-start | bytes 49156 | tf_op jit(solution)/shard_map/while
  239.7 13.3 %copy-start.10 = (f32[16,256]{1,0:T(8,128)}, f32[16,256]{1,0:T(8,128)S(1)}, u32[]{:S(2)}) copy-start(f32[16,256]{1,0:T(8,128)S(1)} %get-tuple-element.784) | copy-start | bytes 49156 | tf_op jit(solution)/shard_map/while
  265.1 13.3 %copy-start.10 = (f32[16,256]{1,0:T(8,128)}, f32[16,256]{1,0:T(8,128)S(1)}, u32[]{:S(2)}) copy-start(f32[16,256]{1,0:T(8,128)S(1)} %get-tuple-element.784) | copy-start | bytes 49156 | tf_op jit(solution)/shard_map/while
  290.5 13.3 %copy-start.10 = (f32[16,256]{1,0:T(8,128)}, f32[16,256]{1,0:T(8,128)S(1)}, u32[]{:S(2)}) copy-start(f32[16,256]{1,0:T(8,128)S(1)} %get-tuple-element.784) | copy-start | bytes 49156 | tf_op jit(solution)/shard_map/while
  316.0 13.3 %copy-start.10 = (f32[16,256]{1,0:T(8,128)}, f32[16,256]{1,0:T(8,128)S(1)}, u32[]{:S(2)}) copy-start(f32[16,256]{1,0:T(8,128)S(1)} %get-tuple-element.784) | copy-start | bytes 49156 | tf_op jit(solution)/shard_map/while
  341.4 13.3 %copy-start.10 = (f32[16,256]{1,0:T(8,128)}, f32[16,256]{1,0:T(8,128)S(1)}, u32[]{:S(2)}) copy-start(f32[16,256]{1,0:T(8,128)S(1)} %get-tuple-element.784) | copy-start | bytes 49156 | tf_op jit(solution)/shard_map/while
  366.8 13.3 %copy-start.10 = (f32[16,256]{1,0:T(8,128)}, f32[16,256]{1,0:T(8,128)S(1)}, u32[]{:S(2)}) copy-start(f32[16,256]{1,0:T(8,128)S(1)} %get-tuple-element.784) | copy-start | bytes 49156 | tf_op jit(solution)/shard_map/while
  392.3 13.3 %copy-start.10 = (f32[16,256]{1,0:T(8,128)}, f32[16,256]{1,0:T(8,128)S(1)}, u32[]{:S(2)}) copy-start(f32[16,256]{1,0:T(8,128)S(1)} %get-tuple-element.784) | copy-start | bytes 49156 | tf_op jit(solution)/shard_map/while
  417.7 13.3 %copy-start.10 = (f32[16,256]{1,0:T(8,128)}, f32[16,256]{1,0:T(8,128)S(1)}, u32[]{:S(2)}) copy-start(f32[16,256]{1,0:T(8,128)S(1)} %get-tuple-element.784) | copy-start | bytes 49156 | tf_op jit(solution)/shard_map/while
  442.5 13.3 %copy-start.10 = (f32[16,256]{1,0:T(8,128)}, f32[16,256]{1,0:T(8,128)S(1)}, u32[]{:S(2)}) copy-start(f32[16,256]{1,0:T(8,128)S(1)} %get-tuple-element.784) | copy-start | bytes 49156 | tf_op jit(solution)/shard_map/while
  467.9 13.3 %copy-start.10 = (f32[16,256]{1,0:T(8,128)}, f32[16,256]{1,0:T(8,128)S(1)}, u32[]{:S(2)}) copy-start(f32[16,256]{1,0:T(8,128)S(1)} %get-tuple-element.784) | copy-start | bytes 49156 | tf_op jit(solution)/shard_map/while
  493.3 13.3 %copy-start.10 = (f32[16,256]{1,0:T(8,128)}, f32[16,256]{1,0:T(8,128)S(1)}, u32[]{:S(2)}) copy-start(f32[16,256]{1,0:T(8,128)S(1)} %get-tuple-element.784) | copy-start | bytes 49156 | tf_op jit(solution)/shard_map/while
  518.8 13.3 %copy-start.10 = (f32[16,256]{1,0:T(8,128)}, f32[16,256]{1,0:T(8,128)S(1)}, u32[]{:S(2)}) copy-start(f32[16,256]{1,0:T(8,128)S(1)} %get-tuple-element.784) | copy-start | bytes 49156 | tf_op jit(solution)/shard_map/while
  (144 other events, 426.0 us)
Sparse Core Ops, SparseCore 0:
  10.7 70.3 all-gather.4
  83.8 51.1 all-gather.6
  544.4 82.6 reduce-scatter.1
where the time goes:
time: 640 us; the launch traced here: 635 us
  waiting for transfers between devices  198 us (31%)
  other arithmetic  142 us (22%)
  local copies, waits for them, and re-layouts  137 us (21%)
  loops' own time  91.4 us (14%)
  matrix products  51.3 us (8%)
  between operations  13.8 us (2%)
    another operation x1, loops' own time, sweep_keys(): return lax.fori_loop(0, block_count, sweep_turn, (query_init, keys_init))  88.3 us
    reduce_scatter x1, waiting for transfers between devices, body(): lax.psum_scatter(key_value_full.astype(jnp.bfloat16), 'ctx', scatter_dime...  79.1 us
    all_gather x1, waiting for transfers between devices, body(): lax.all_gather(value_block, 'ctx', axis=0, tiled=True)  53.9 us
    while x320, local copies, waits for them, and re-layouts  44.6 us
    all_gather x1, waiting for transfers between devices, body(): lax.all_gather(key_block, 'ctx', axis=0, tiled=True)  44 us
    add x32, other arithmetic, sweep_turn(): query_sum = query_sum + tile_out[0]  42.8 us
    slice x16, other arithmetic, sweep_turn(): query_pos[row_low:row_high]  31.5 us
    le x33, other arithmetic, tile_grads(): allowed = key_pos[None, :] <= query_pos[:, None]  23.8 us
  transfers between devices with their start and end apart: 4, of which 4 were waited for; matrix products, arithmetic and copies ran while one was open for 1% of the time, Pallas kernels for 0%

commit v1 on v0

--- a/solution.py
+++ b/solution.py
@@ -141,7 +141,9 @@
     query_side = (query_block, grad_out, lse[0], delta_rows, query_pos, own_starts, span_start)
     query_add, key_value_part = sweep_keys(
         query_side,
-        lax.all_gather(key_block, "ctx", axis=0, tiled=True),
+        jnp.concatenate(
+            lax.all_to_all(jnp.stack([key_block] * lax.axis_size("ctx")), "ctx", 0, 0), axis=0
+        ),
         lax.all_gather(value_block, "ctx", axis=0, tiled=True),
     )
     key_value_full = key_value_part

time: 640 us -> 578 us (0.903)
  waiting for transfers between devices: 198 us -> 137 us
  starting transfers between devices: 2.36 us -> 12 us
  loops' own time: 91.4 us -> 83.9 us
    all_gather x1 -> x0, waiting for transfers between devices: 44 us -> none  [body(): lax.all_gather(key_block, 'ctx', axis=0, tiled=True)]
    all_gather x1, waiting for transfers between devices: 53.9 us -> 24.5 us  [body(): lax.all_gather(value_block, 'ctx', axis=0, tiled=True)]
    all_to_all x0 -> x1, starting transfers between devices: none -> 11.4 us  [body(): lax.all_to_all(jnp.stack([key_block] * lax.axis_size('ctx')), 'ctx', 0, 0)]
    reduce_scatter x1, waiting for transfers between devices: 79.1 us -> 90.3 us  [body(): lax.psum_scatter(key_value_full.astype(jnp.bfloat16), 'ctx', scatter_dime...]
    another operation x1, loops' own time: 88.3 us -> 80.8 us  [sweep_keys(): return lax.fori_loop(0, block_count, sweep_turn, (query_init, keys_init))]
  transfers between devices with their start and end apart: 4 -> 4, of which waited for: 4 -> 3; matrix products, arithmetic and copies ran while one was open for 1% -> 2% of each run, Pallas kernels for 0% -> 0%
where the time goes in v1:
time: 578 us; the launch traced here: 573 us
  other arithmetic  141 us (24%)
  waiting for transfers between devices  137 us (24%)
  local copies, waits for them, and re-layouts  134 us (23%)
  loops' own time  83.9 us (15%)
  matrix products  51.4 us (9%)
  between operations  14.1 us (2%)
  starting transfers between devices  12 us (2%)
    reduce_scatter x1, waiting for transfers between devices, body(): lax.psum_scatter(key_value_full.astype(jnp.bfloat16), 'ctx', scatter_dime...  90.3 us
    another operation x1, loops' own time, sweep_keys(): return lax.fori_loop(0, block_count, sweep_turn, (query_init, keys_init))  80.8 us
    add x32, other arithmetic, sweep_turn(): query_sum = query_sum + tile_out[0]  43.5 us
    while x320, local copies, waits for them, and re-layouts  41.3 us
    slice x16, other arithmetic, sweep_turn(): query_pos[row_low:row_high]  30.2 us
    all_gather x1, waiting for transfers between devices, body(): lax.all_gather(value_block, 'ctx', axis=0, tiled=True)  24.5 us
    le x33, other arithmetic, tile_grads(): allowed = key_pos[None, :] <= query_pos[:, None]  22.5 us
    slice x16, local copies, waits for them, and re-layouts, sweep_turn(): grad_out[row_low:row_high]  21.5 us
  transfers between devices with their start and end apart: 4, of which 3 were waited for; matrix products, arithmetic and copies ran while one was open for 2% of the time, Pallas kernels for 0%

profile of v1, /device:TPU:2, one launch (start us, length us, event | category | flops | bytes accessed | tf_op | source)
XLA Modules:
  0.0 572.9 jit_solution(7990362391594796757)
XLA Ops:
  9.9 11.4 %all-to-all-start = ((bf16[16,256,128]{2,1,0:T(8,128)(2,1)}), bf16[16,256,128]{2,1,0:T(8,128)(2,1)}, u32[]{:S(2)}, u32[]{:S(2)}) async-start(bf16[16,256,128]{2,1,0:T(8,128)(2,1)} %stack.3), calls=%async_computation | async-start | bytes 2097152 | tf_op jit(solution)/shard_map/all_to_all | solution.py:145
  26.9 21.3 %collective-permute-done = bf16[1,256,16,128]{3,1,2,0:T(8,128)(2,1)S(1)} collective-permute-done((bf16[1,256,16,128]{3,1,2,0:T(8,128)(2,1)}, bf16[1,256,16,128]{3,1,2,0:T(8,128)(2,1)S(1)}, u32[]{:S(2)}, u32[]{:S(2)}) %collective-permute-start) | collective-permute-done | bytes 1048608 | tf_op jit(solution)/shard_map/ppermute | solution.py:9
  50.1 24.5 %all-gather.3.cloned.1.call-done = bf16[1,4096,128]{2,1,0:T(8,128)(2,1)} async-done(((bf16[1,256,128]{2,1,0:T(8,128)(2,1)}), bf16[1,4096,128]{2,1,0:T(8,128)(2,1)}) %all-gather.3.cloned.1.call-update) | async-done | bytes 1048592 | tf_op jit(solution)/shard_map/all_gather | solution.py:147
  76.1 394.3 %while.19 = (s32[]{:T(128)}, f32[256,16,128]{2,0,1:T(8,128)}, bf16[4096,256]{1,0:T(8,128)(2,1)}, s32[32]{0:T(128)}, s32[2]{0:T(128)}, /*index=5*/bf16[4096,128]{...) while((s32[]{:T(128)}, f32[256,16,128]{2,0,1:T(8,128)}, ...), condition=%wide.region_10.11_spmd.clone.clone, body=%wide.region_1.10_spmd.clone.clone.sunk | while | flops 1353384192 | bytes 84388064 | solution.py:124
  93.0 2.4 conditional.16
  95.4 2.3 conditional.17
  117.6 2.4 conditional.16
  142.1 2.4 conditional.16
  166.7 2.4 conditional.16
  191.3 2.4 conditional.16
  215.9 2.4 conditional.16
  240.5 2.4 conditional.16
  265.1 2.4 conditional.16
  289.7 2.4 conditional.16
  314.3 2.4 conditional.16
  338.9 2.4 conditional.16
  341.3 2.3 conditional.17
  365.0 2.4 conditional.16
  387.5 2.4 conditional.16
  412.0 2.4 conditional.16
  436.6 2.4 conditional.16
  439.0 2.3 conditional.17
  461.2 2.4 conditional.16
  474.3 90.3 %reduce-scatter.2.cloned.1.call-done = bf16[256,256]{1,0:T(8,128)(2,1)} async-done(((bf16[4096,256]{1,0:T(8,128)(2,1)}), bf16[256,256]{1,0:T(8,128)(2,1)}) %reduce-scatter.2.cloned.1.call-update) | async-done | bytes 131088 | tf_op jit(solution)/shard_map/reduce_scatter | solution.py:151
  (936 shorter events, 362.8 us)
Async XLA Ops:
  7.2 14.2 %copy-start.8 = (bf16[1,256,16,128]{3,2,1,0:T(8,128)(2,1)S(1)}, bf16[1,256,16,128]{3,2,1,0:T(8,128)(2,1)}, u32[]{:S(2)}) copy-start(bf16[1,256,16,128]{3,2,1,0:T(8,128)(2,1)} %param.21) | copy-start | bytes 3145732
  7.2 67.5 %all-gather.3.cloned.1.call-start = ((), (), s32[]{:S(2)}) async-start(), calls=%async_computation.3 | async-start | bytes 1114112 | tf_op jit(solution)/shard_map/all_gather | solution.py:147
  9.9 13.3 %copy-start.9 = (bf16[1,256,16,128]{3,2,1,0:T(8,128)(2,1)S(1)}, bf16[1,256,16,128]{3,2,1,0:T(8,128)(2,1)}, u32[]{:S(2)}) copy-start(bf16[1,256,16,128]{3,2,1,0:T(8,128)(2,1)} %param.17) | copy-start | bytes 3145732
  9.9 64.7 %all-to-all-start = ((bf16[16,256,128]{2,1,0:T(8,128)(2,1)}), bf16[16,256,128]{2,1,0:T(8,128)(2,1)}, u32[]{:S(2)}, u32[]{:S(2)}) async-start(bf16[16,256,128]{2,1,0:T(8,128)(2,1)} %stack.3), calls=%async_computation | async-start | bytes 2097152 | tf_op jit(solution)/shard_map/all_to_all | solution.py:145
  21.3 543.2 %reduce-scatter.2.cloned.1.call-start = ((), (), s32[]{:S(2)}) async-start(), calls=%async_computation.2 | async-start | bytes 2228224 | tf_op jit(solution)/shard_map/reduce_scatter | solution.py:151
  22.6 25.6 %collective-permute-start = (bf16[1,256,16,128]{3,1,2,0:T(8,128)(2,1)}, bf16[1,256,16,128]{3,1,2,0:T(8,128)(2,1)S(1)}, u32[]{:S(2)}, u32[]{:S(2)}) collective-permute-start(bf16[1,256,16,128]{3,1,2,0:T(8,128)(2,1)} %copy.15), channel_id=1, source_target_pairs={{0,240},{16,0},{32,16},{48,32},{64,48},{80,64},{96,80},{112,96},{1... | collective-permute-start | bytes 3145736 | tf_op jit(solution)/shard_map/ppermute | solution.py:9
  26.9 49.2 %copy-start.12 = (f32[1,16,256]{2,1,0:T(8,128)S(1)}, f32[1,16,256]{2,1,0:T(8,128)}, u32[]{:S(2)}) copy-start(f32[1,16,256]{2,1,0:T(8,128)} %param.22) | copy-start | bytes 49156
  102.2 12.7 %copy-start.5 = (bf16[256,16,128]{2,0,1:T(8,128)(2,1)}, bf16[256,16,128]{2,0,1:T(8,128)(2,1)S(1)}, u32[]{:S(2)}) copy-start(bf16[256,16,128]{2,0,1:T(8,128)(2,1)S(1)} %get-tuple-element.783) | copy-start | bytes 3145732 | tf_op jit(solution)/shard_map/while
  102.2 12.7 %copy-start.10 = (f32[16,256]{1,0:T(8,128)}, f32[16,256]{1,0:T(8,128)S(1)}, u32[]{:S(2)}) copy-start(f32[16,256]{1,0:T(8,128)S(1)} %get-tuple-element.784) | copy-start | bytes 49156 | tf_op jit(solution)/shard_map/while
  126.8 12.7 %copy-start.5 = (bf16[256,16,128]{2,0,1:T(8,128)(2,1)}, bf16[256,16,128]{2,0,1:T(8,128)(2,1)S(1)}, u32[]{:S(2)}) copy-start(bf16[256,16,128]{2,0,1:T(8,128)(2,1)S(1)} %get-tuple-element.783) | copy-start | bytes 3145732 | tf_op jit(solution)/shard_map/while
  126.8 12.7 %copy-start.10 = (f32[16,256]{1,0:T(8,128)}, f32[16,256]{1,0:T(8,128)S(1)}, u32[]{:S(2)}) copy-start(f32[16,256]{1,0:T(8,128)S(1)} %get-tuple-element.784) | copy-start | bytes 49156 | tf_op jit(solution)/shard_map/while
  151.4 12.7 %copy-start.10 = (f32[16,256]{1,0:T(8,128)}, f32[16,256]{1,0:T(8,128)S(1)}, u32[]{:S(2)}) copy-start(f32[16,256]{1,0:T(8,128)S(1)} %get-tuple-element.784) | copy-start | bytes 49156 | tf_op jit(solution)/shard_map/while
  176.0 12.7 %copy-start.10 = (f32[16,256]{1,0:T(8,128)}, f32[16,256]{1,0:T(8,128)S(1)}, u32[]{:S(2)}) copy-start(f32[16,256]{1,0:T(8,128)S(1)} %get-tuple-element.784) | copy-start | bytes 49156 | tf_op jit(solution)/shard_map/while
  200.6 12.7 %copy-start.10 = (f32[16,256]{1,0:T(8,128)}, f32[16,256]{1,0:T(8,128)S(1)}, u32[]{:S(2)}) copy-start(f32[16,256]{1,0:T(8,128)S(1)} %get-tuple-element.784) | copy-start | bytes 49156 | tf_op jit(solution)/shard_map/while
  225.2 12.7 %copy-start.10 = (f32[16,256]{1,0:T(8,128)}, f32[16,256]{1,0:T(8,128)S(1)}, u32[]{:S(2)}) copy-start(f32[16,256]{1,0:T(8,128)S(1)} %get-tuple-element.784) | copy-start | bytes 49156 | tf_op jit(solution)/shard_map/while
  249.7 12.7 %copy-start.10 = (f32[16,256]{1,0:T(8,128)}, f32[16,256]{1,0:T(8,128)S(1)}, u32[]{:S(2)}) copy-start(f32[16,256]{1,0:T(8,128)S(1)} %get-tuple-element.784) | copy-start | bytes 49156 | tf_op jit(solution)/shard_map/while
  274.3 12.7 %copy-start.10 = (f32[16,256]{1,0:T(8,128)}, f32[16,256]{1,0:T(8,128)S(1)}, u32[]{:S(2)}) copy-start(f32[16,256]{1,0:T(8,128)S(1)} %get-tuple-element.784) | copy-start | bytes 49156 | tf_op jit(solution)/shard_map/while
  298.9 12.7 %copy-start.10 = (f32[16,256]{1,0:T(8,128)}, f32[16,256]{1,0:T(8,128)S(1)}, u32[]{:S(2)}) copy-start(f32[16,256]{1,0:T(8,128)S(1)} %get-tuple-element.784) | copy-start | bytes 49156 | tf_op jit(solution)/shard_map/while
  323.5 12.7 %copy-start.10 = (f32[16,256]{1,0:T(8,128)}, f32[16,256]{1,0:T(8,128)S(1)}, u32[]{:S(2)}) copy-start(f32[16,256]{1,0:T(8,128)S(1)} %get-tuple-element.784) | copy-start | bytes 49156 | tf_op jit(solution)/shard_map/while
  348.1 12.7 %copy-start.10 = (f32[16,256]{1,0:T(8,128)}, f32[16,256]{1,0:T(8,128)S(1)}, u32[]{:S(2)}) copy-start(f32[16,256]{1,0:T(8,128)S(1)} %get-tuple-element.784) | copy-start | bytes 49156 | tf_op jit(solution)/shard_map/while
  372.1 12.7 %copy-start.10 = (f32[16,256]{1,0:T(8,128)}, f32[16,256]{1,0:T(8,128)S(1)}, u32[]{:S(2)}) copy-start(f32[16,256]{1,0:T(8,128)S(1)} %get-tuple-element.784) | copy-start | bytes 49156 | tf_op jit(solution)/shard_map/while
  396.7 12.7 %copy-start.10 = (f32[16,256]{1,0:T(8,128)}, f32[16,256]{1,0:T(8,128)S(1)}, u32[]{:S(2)}) copy-start(f32[16,256]{1,0:T(8,128)S(1)} %get-tuple-element.784) | copy-start | bytes 49156 | tf_op jit(solution)/shard_map/while
  421.3 12.7 %copy-start.10 = (f32[16,256]{1,0:T(8,128)}, f32[16,256]{1,0:T(8,128)S(1)}, u32[]{:S(2)}) copy-start(f32[16,256]{1,0:T(8,128)S(1)} %get-tuple-element.784) | copy-start | bytes 49156 | tf_op jit(solution)/shard_map/while
  445.9 12.7 %copy-start.10 = (f32[16,256]{1,0:T(8,128)}, f32[16,256]{1,0:T(8,128)S(1)}, u32[]{:S(2)}) copy-start(f32[16,256]{1,0:T(8,128)S(1)} %get-tuple-element.784) | copy-start | bytes 49156 | tf_op jit(solution)/shard_map/while
  (144 other events, 420.1 us)
Sparse Core Ops, SparseCore 0:
  10.7 63.9 all-gather.2
  470.6 93.8 reduce-scatter.1
